TPU v7x, 32 devices: a whole 2x2x4 slice. The times are simulated.
32 devices in a mesh: groups: 2 (over y), seq: 4 (over z), mp: 2 (over x), section: 2 (over core).
Axes of the slice: x: 2, y: 2, z: 4, core: 2. Of those that a mesh axis runs over, the one named last changes fastest.
Arguments:
- features: bfloat16 [4, 512, 8192], P(('groups', 'section'), 'mp', 'seq'), parts along dimension 0, may hold values from -6 to 6
- alpha: float32 [512], P('mp'), may hold values from 0.5 to 2
- conv_weight: bfloat16 [1024, 32, 16], P('mp'), may hold values from -0.25 to 0.25
- qkv_weight: bfloat16 [1024, 3, 1024], P(None, None, 'mp'), may hold values from -1 to 1
- readout: float32 [1024], P('mp'), may hold values from -4 to 4
- offsets: int32 [4], P(('groups', 'section')), parts along dimension 0, may hold values from 0 to 14479
- pairs: int32 [8, 2], P('groups'), parts along dimension 0, may hold values from 0 to 1
- labels: int32 [8], P('groups'), parts along dimension 0, may hold values from 0 to 1
Outputs:
- grads: bfloat16 [3, 4, 1024, 1024], P(None, ('groups', 'section'), 'seq', 'mp'), parts along dimension 1
- rewards: float32 [4], P('groups'), parts along dimension 0
- loss: float32 [2], P('groups'), parts along dimension 0
There are 2 independent parts, one for each index of `groups`. A program takes and returns all parts, laid end to end along the dimension named above; an argument that names none is the same for every part. Nothing has to cross between parts.
All inputs are finite; a program needn't handle non-finite values.
Results may differ from a plain program's by a relative error of at most 0.017.
Values may be sent and summed in bfloat16 or wider, within the bound.
A program may use at most 64 MiB of HBM per device.

v0:
```python
import math
import jax
import jax.numpy as jnp
from jax import lax
from jax.sharding import PartitionSpec as P

D = 1024
HD = 64
EPS = 1e-06
BASE = 10000.0


def padded_2(block, sides, width):
    for axis, dim in sides:
        count = lax.axis_size(axis)
        forward = [(i, i + 1) for i in range(count - 1)]
        backward = [(target, source) for source, target in forward]
        low = lax.ppermute(
            lax.slice_in_dim(block, block.shape[dim] - width, None, axis=dim), axis, forward
        )
        high = lax.ppermute(lax.slice_in_dim(block, 0, width, axis=dim), axis, backward)
        block = jnp.concatenate([low, block, high], axis=dim)
    return block


def position_table(positions, feature_ids, width):
    pair_ids = (feature_ids // 2).astype(jnp.float32)
    freqs = jnp.exp(pair_ids * (-2.0 * math.log(BASE) / width))
    angle = positions.astype(jnp.float32)[..., None] * freqs
    return jnp.where(feature_ids % 2 == 0, jnp.sin(angle), jnp.cos(angle))


def local(features, alpha, conv_weight, qkv_weight, readout, offsets, pairs, labels):
    f32 = jnp.float32
    bf16 = jnp.bfloat16
    cand, chans, samples = features.shape
    local_width = conv_weight.shape[0]
    per_group = conv_weight.shape[1]
    kern = conv_weight.shape[2]
    stride = kern // 2
    frames_dev = samples // stride
    groups_here = chans // per_group
    heads_here = local_width // HD
    raw = features.astype(f32)
    slope = alpha[None, :, None]
    act = (raw + jnp.sin(slope * raw) ** 2 / slope).astype(bf16)
    padded = padded_2(act, (("seq", 2),), stride // 2)
    blocks = padded.reshape(cand, groups_here, per_group, frames_dev + 1, stride).transpose(
        0, 1, 3, 2, 4
    )
    patches = jnp.concatenate([blocks[:, :, :-1], blocks[:, :, 1:]], axis=-1).reshape(
        cand, groups_here, frames_dev, per_group * kern
    )
    kernel = conv_weight.reshape(groups_here, local_width // groups_here, per_group * kern)
    frames = jnp.einsum("cgfk,gok->cfgo", patches, kernel, preferred_element_type=f32).reshape(
        cand, frames_dev, local_width
    )
    slice_id = lax.axis_index("seq")
    part_id = lax.axis_index("mp")
    positions = (
        offsets[:, None] + slice_id * frames_dev + jnp.arange(frames_dev, dtype=jnp.int32)[None, :]
    )
    feature_ids = part_id * local_width + jnp.arange(local_width, dtype=jnp.int32)
    resid = (frames + position_table(positions, feature_ids, D)).astype(bf16)
    whole = lax.all_gather(resid, "mp", axis=2, tiled=True)
    squares = jnp.mean(jnp.square(whole.astype(f32)), axis=-1)
    projected = jnp.einsum("cfd,dtk->cftk", whole, qkv_weight, preferred_element_type=f32)
    qkv = (projected * lax.rsqrt(squares + EPS)[:, :, None, None]).astype(bf16)
    query = qkv[:, :, 0]
    keys, values = (
        lax.all_gather(qkv[:, :, 1], "seq", axis=1, tiled=True),
        lax.all_gather(qkv[:, :, 2], "seq", axis=1, tiled=True),
    )
    total = keys.shape[1]
    block = min(512, total)
    count_blocks = total // block
    scale = 1.0 / math.sqrt(HD)
    query4 = query.reshape(cand, frames_dev, heads_here, HD)

    def key_slice(source, start, size):
        return lax.dynamic_slice_in_dim(source, start, size, 1).reshape(cand, size, heads_here, HD)

    def scores_for(start, size):
        return (
            jnp.einsum(
                "cfhe,ckhe->chfk", query4, key_slice(keys, start, size), preferred_element_type=f32
            )
            * scale
        )

    def stat_step(carry, index):
        peak_now, mass_now = carry
        score = scores_for(index * block, block)
        fresh = jnp.maximum(peak_now, jnp.max(score, axis=-1))
        mass_now = mass_now * jnp.exp(peak_now - fresh) + jnp.sum(
            jnp.exp(score - fresh[..., None]), axis=-1
        )
        return ((fresh, mass_now), None)

    start_peak = jnp.full((cand, heads_here, frames_dev), -jnp.inf, f32)
    (peak, mass), _ = lax.scan(
        stat_step, (start_peak, jnp.zeros_like(start_peak)), jnp.arange(count_blocks)
    )

    def weights_for(start, size):
        return jnp.exp(scores_for(start, size) - peak[..., None]) / mass[..., None]

    def out_step(running, index):
        start = index * block
        prob = weights_for(start, block).astype(bf16)
        running = running + jnp.einsum(
            "chfk,ckhe->cfhe", prob, key_slice(values, start, block), preferred_element_type=f32
        )
        return (running, None)

    attended4, _ = lax.scan(
        out_step, jnp.zeros((cand, frames_dev, heads_here, HD), f32), jnp.arange(count_blocks)
    )
    attended = attended4.reshape(cand, frames_dev, local_width)
    gate = jax.nn.sigmoid(lax.optimization_barrier(resid).astype(f32))
    section_id = lax.axis_index("section")
    all_cands = cand * lax.axis_size("section")
    owner = (
        jnp.arange(all_cands, dtype=jnp.int32)[None, :]
        == (section_id * cand + jnp.arange(cand, dtype=jnp.int32))[:, None]
    ).astype(f32)
    partial_rewards = jnp.sum(attended * gate * readout, axis=(1, 2)) / math.sqrt(total)
    rewards = lax.psum(jnp.sum(owner * partial_rewards[:, None], axis=0), ("seq", "mp", "section"))
    chosen = (pairs[:, :, None] == jnp.arange(all_cands, dtype=jnp.int32)[None, None, :]).astype(
        f32
    )
    paired = jnp.sum(chosen * rewards[None, None, :], axis=-1)
    margin = paired[:, 0] - paired[:, 1]
    target = labels.astype(f32)
    loss = jnp.sum(jax.nn.softplus(margin) - target * margin)
    coeff = jax.nn.sigmoid(margin) - target
    reward_grad = jnp.sum(coeff[:, None] * (chosen[:, 0] - chosen[:, 1]), axis=0)
    own_grad = jnp.sum(owner * reward_grad[None, :], axis=1)
    upstream = (own_grad[:, None, None] * readout * gate).astype(bf16)
    upstream4 = upstream.reshape(cand, frames_dev, heads_here, HD)
    delta = jnp.sum(upstream4.astype(f32) * attended4, axis=-1).transpose(0, 2, 1)

    def backward_block(start, size):
        prob = weights_for(start, size)
        prob_low = prob.astype(bf16)
        dprob = jnp.einsum(
            "cfhe,ckhe->chfk", upstream4, key_slice(values, start, size), preferred_element_type=f32
        )
        dscore = (prob * (dprob - delta[..., None])).astype(bf16)
        dquery = (
            jnp.einsum(
                "chfk,ckhe->cfhe", dscore, key_slice(keys, start, size), preferred_element_type=f32
            )
            * scale
        )
        dkey = jnp.einsum("chfk,cfhe->kche", dscore, query4, preferred_element_type=f32) * scale
        dvalue = jnp.einsum("chfk,cfhe->kche", prob_low, upstream4, preferred_element_type=f32)
        term = jnp.concatenate(
            [dkey.reshape(size, cand, local_width), dvalue.reshape(size, cand, local_width)],
            axis=-1,
        )
        return (dquery, term)

    zero_query = jnp.zeros((cand, frames_dev, heads_here, HD), f32)

    def grad_step(running, index):
        dquery, term = backward_block(index * block, block)
        return (running + dquery, term.astype(bf16))

    grad_query, stored = lax.scan(grad_step, zero_query, jnp.arange(count_blocks))
    stacked = stored.reshape(total, cand, 2 * local_width)
    summed = lax.psum_scatter(
        stacked.astype(f32).astype(jnp.bfloat16), "seq", scatter_dimension=0, tiled=True
    ).astype(jnp.float32)
    grad_key = summed[:, :, :local_width].transpose(1, 0, 2)
    grad_value = summed[:, :, local_width:].transpose(1, 0, 2)
    grads = jnp.stack(
        [grad_query.reshape(cand, frames_dev, local_width), grad_key, grad_value], axis=0
    ).astype(bf16)
    return (grads, rewards, loss.reshape(1))


def solution(mesh):
    placed = (
        P(("groups", "section"), "mp", "seq"),
        P("mp"),
        P("mp", None, None),
        P(None, None, "mp"),
        P("mp"),
        P(("groups", "section")),
        P("groups", None),
        P("groups"),
    )
    return jax.shard_map(
        local,
        mesh=mesh,
        in_specs=placed,
        out_specs=(P(None, ("groups", "section"), "seq", "mp"), P("groups"), P("groups")),
        check_vma=False,
    )
```

profile of v0, /device:TPU:0, one launch (start us, length us, event | category | flops | bytes accessed | tf_op | source)
XLA Modules:
  0.0 278.7 jit_solution(6267920341593110061)
XLA Ops:
  7.2 8.6 %fusion.25 = bf16[1,256,2048]{2,1,0:T(8,128)(2,1)S(1)} fusion(bf16[1,256,2048]{2,1,0:T(8,128)(2,1)} %param.14, f32[256]{0:T(256)} %param.15), kind=kLoop, calls=%fused_computation.40 | loop fusion | flops 3145728 | bytes 2098176 | tf_op jit(solution)/shard_map/convert_element_type | solution.py:46
  17.0 4.9 %collective-permute-start = (bf16[1,256,4]{2,1,0:T(8,128)(2,1)S(1)}, bf16[1,256,4]{2,1,0:T(8,128)(2,1)S(1)}, u32[]{:S(2)}, u32[]{:S(2)}) collective-permute-start(bf16[1,256,4]{2,1,0:T(8,128)(2,1)S(1)} %get-tuple-element.365), channel_id=1, source_target_pairs={{0,4},{4,8},{8,12},{1,5},{5,9},{9,13},{2,6},{6,10},{10,14},{3,7},{... | collective-permute-start | bytes 6152 | tf_op jit(solution)/shard_map/ppermute | solution.py:18
  21.9 1.5 collective-permute-start.1
  24.1 2.4 reshape.438
  26.5 1.5 collective-permute-done.1
  28.1 3.5 %concatenate.32 = bf16[1,256,2056]{2,1,0:T(8,128)(2,1)} concatenate(bf16[1,256,4]{2,1,0:T(8,128)(2,1)S(1)} %collective-permute-done, bf16[1,256,2048]{2,1,0:T(8,128)(2,1)} %copy-done.5, bf16[1,256,4]{2,1,0:T(8,128)(2,1)S(1)} %collective-permute-done.1), dimensions={2} | concatenate | bytes 2105344 | tf_op jit(solution)/shard_map/concatenate | solution.py:22
  31.6 2.3 copy.41
  33.9 5.8 %reshape.436 = bf16[1,8,32,257,8]{2,1,4,3,0:T(8,128)(2,1)} reshape(bf16[1,256,2056]{1,2,0:T(8,128)(2,1)} %copy.41) | data formatting | bytes 2105344 | tf_op jit(solution)/shard_map/reshape | solution.py:48
  39.7 6.5 %fusion.53 = (bf16[1,8,256,32,8]{3,1,4,2,0:T(8,128)(2,1)}, bf16[1,8,256,32,8]{3,1,4,2,0:T(8,128)(2,1)}) fusion(bf16[1,8,257,32,8]{3,1,4,2,0:T(8,128)(2,1)} %bitcast.233), kind=kLoop, calls=%fused_computation.102 | loop fusion | bytes 4194304 | tf_op jit(solution)/shard_map/slice | solution.py:51
  46.2 7.7 %copy.42 = bf16[1,8,256,32,8]{2,4,3,1,0:T(8,128)(2,1)} copy(bf16[1,8,256,32,8]{3,1,4,2,0:T(8,128)(2,1)} %get-tuple-element.362) | data formatting | bytes 2097152 | tf_op jit(solution)/shard_map/slice | solution.py:51
  53.9 7.7 %copy.43 = bf16[1,8,256,32,8]{2,4,3,1,0:T(8,128)(2,1)} copy(bf16[1,8,256,32,8]{3,1,4,2,0:T(8,128)(2,1)} %get-tuple-element.363) | data formatting | bytes 2097152 | tf_op jit(solution)/shard_map/slice | solution.py:51
  61.7 1.8 pad_maximum_fusion
  63.5 1.3 fusion.27
  64.9 2.0 copy.46
  66.9 3.5 %fusion.31 = bf16[1,256,512]{2,1,0:T(8,128)(2,1)S(1)} fusion(f32[1,256,512]{2,1,0:T(8,128)} %copy.46, f32[512]{0:T(512)S(1)} %fusion.36, f32[256]{0:T(256)S(1)} %add_convert_fusion, pred[512]{0:T(512)(128)(4,1)S(1)} %fusion.33), kind=kLoop, calls=%fused_computation.52 | loop fusion | flops 524288 | bytes 790016 | tf_op jit(solution)/shard_map/convert_element_type | solution.py:64
  71.1 7.3 %all_gather.9 = bf16[1,256,1024]{2,1,0:T(8,128)(2,1)S(1)} all-gather(bf16[1,256,512]{2,1,0:T(8,128)(2,1)S(1)} %fusion.31), channel_id=1, replica_groups=mesh['groups'=2,'seq'=4,'mp'=2,'section'=2] {'mp'}, dimensions={2}, use_global_device_ids=true | all-gather | bytes 786432 | tf_op jit(solution)/shard_map/all_gather | solution.py:65
  80.7 1.1 copy.47
  82.1 28.3 %all-gather.5.cloned.1.call-done = bf16[1,1024,1,512]{3,1,2,0:T(8,128)(2,1)} async-done(((bf16[1,256,1,512]{3,1,2,0:T(8,128)(2,1)}), bf16[1,1024,1,512]{3,1,2,0:T(8,128)(2,1)}) %all-gather.5.cloned.1.call-update) | async-done | bytes 1048592 | tf_op jit(solution)/shard_map/all_gather | solution.py:71
  110.4 2.3 copy.53
  112.6 16.1 %while.37 = (s32[]{:T(128)}, f32[1,8,256]{2,1,0:T(8,128)S(1)}, f32[1,8,256]{2,1,0:T(8,128)S(1)}, s32[2]{0:T(128)S(1)}, bf16[1,1024,512]{1,2,0:T(8,128)(2,1)}, /*...) while((s32[]{:T(128)}, f32[1,8,256]{2,1,0:T(8,128)S(1)}, ...), condition=%wide.region_4.5_spmd.clone, body=%wide.region_1.4_spmd.clone.sunk | while | flops 139470848 | bytes 10330286 | solution.py:101
  115.0 2.7 bitcast_reduce_fusion.2
  117.7 3.0 %fusion.86 = f32[8,256]{1,0:T(8,128)S(1)} fusion(f32[8,512,256]{2,1,0:T(8,128)} %get-tuple-element.514, f32[8,256]{1,0:T(8,128)S(1)} %bitcast.239), kind=kLoop, calls=%fused_computation.3.clone.1 | loop fusion | flops 3143680 | bytes 4210688 | tf_op jit(solution)/shard_map/while/body/eval_jaxpr/reduce_sum | solution.py:95
  123.1 2.7 bitcast_reduce_fusion.2
  125.8 2.9 %fusion.86 = f32[8,256]{1,0:T(8,128)S(1)} fusion(f32[8,512,256]{2,1,0:T(8,128)} %get-tuple-element.514, f32[8,256]{1,0:T(8,128)S(1)} %bitcast.239), kind=kLoop, calls=%fused_computation.3.clone.1 | loop fusion | flops 3143680 | bytes 4210688 | tf_op jit(solution)/shard_map/while/body/eval_jaxpr/reduce_sum | solution.py:95
  128.7 10.6 %all-gather.7.cloned.1.call-done = bf16[1,1024,1,512]{3,1,2,0:T(8,128)(2,1)} async-done(((bf16[1,256,1,512]{3,1,2,0:T(8,128)(2,1)}), bf16[1,1024,1,512]{3,1,2,0:T(8,128)(2,1)}) %all-gather.7.cloned.1.call-update) | async-done | bytes 1048592 | tf_op jit(solution)/shard_map/all_gather | solution.py:72
  139.4 2.3 copy.54
  141.7 13.9 %while.38 = (s32[]{:T(128)}, f32[1,256,8,64]{1,3,2,0:T(8,128)}, s32[2]{0:T(128)S(1)}, bf16[1,1024,512]{1,2,0:T(8,128)(2,1)}, bf16[1,1024,512]{1,2,0:T(8,128)(2,1...) while((s32[]{:T(128)}, f32[1,256,8,64]{1,3,2,0:T(8,128)}, ...), condition=%wide.region_6.7_spmd.clone, body=%wide.region_5.6_spmd.clone.sunk | while | flops 272891904 | bytes 4473021 | solution.py:116
  142.9 2.3 constant_dynamic-slice_fusion.9
  145.2 3.4 %fusion.90 = f32[1,256,8,64]{1,3,2,0:T(8,128)} fusion(bf16[512,8,64]{0,2,1:T(8,128)(2,1)} %bitcast.236, bf16[512,8,64]{0,2,1:T(8,128)(2,1)} %bitcast.235, f32[8,256]{1,0:T(8,128)S(1)} %bitcast.249, f32[8,256]{1,0:T(8,128)S(1)} %bitcast.245, f32[1,256,8,64]{1,3,2,0:T(8,128)} %get-tuple-element.581, ...), kind=kOutput, calls=%fused_computation.13.clone.1 | convolution fusion | flops 272891904 | bytes 2375681 | tf_op jit(solution)/shard_map/while/body/eval_jaxpr/chfk,ckhe->cfhe/dot_general | solution.py:111
  149.8 2.3 constant_dynamic-slice_fusion.9
  152.0 3.6 %fusion.90 = f32[1,256,8,64]{1,3,2,0:T(8,128)} fusion(bf16[512,8,64]{0,2,1:T(8,128)(2,1)} %bitcast.236, bf16[512,8,64]{0,2,1:T(8,128)(2,1)} %bitcast.235, f32[8,256]{1,0:T(8,128)S(1)} %bitcast.249, f32[8,256]{1,0:T(8,128)S(1)} %bitcast.245, f32[1,256,8,64]{1,3,2,0:T(8,128)} %get-tuple-element.581, ...), kind=kOutput, calls=%fused_computation.13.clone.1 | convolution fusion | flops 272891904 | bytes 2375681 | tf_op jit(solution)/shard_map/while/body/eval_jaxpr/chfk,ckhe->cfhe/dot_general | solution.py:111
  155.6 2.1 copy.51
  157.7 1.9 multiply_reduce_fusion.2
  160.3 31.9 %psum.7 = f32[2]{0:T(128)S(1)} all-reduce(f32[2]{0:T(128)S(1)} %compare_select_fusion.2), channel_id=1, replica_groups=mesh['groups'=2,'seq'=4,'mp'=2,'section'=2] {'seq','mp','section'}, use_global_device_ids=true, to_apply=%region_8.9 | all-reduce | flops 2 | bytes 16 | tf_op jit(solution)/shard_map/psum | solution.py:128
  194.3 1.8 multiply_convert_fusion.2
  197.1 1.1 multiply_reduce_fusion.1
  198.3 25.0 %while.39 = (s32[]{:T(128)}, f32[1,256,8,64]{1,3,2,0:T(8,128)}, bf16[2,512,1,1024]{1,3,2,0:T(8,128)(2,1)}, s32[2]{0:T(128)S(1)}, bf16[1,1024,512]{1,2,0:T(8,128)...) while((s32[]{:T(128)}, f32[1,256,8,64]{1,3,2,0:T(8,128)}, ...), condition=%wide.region_14.15_spmd.clone, body=%wide.region_13.14_spmd.clone.sunk | while | flops 681705472 | bytes 39346984 | solution.py:170
  199.5 1.3 constant_dynamic-slice_fusion.10
  200.8 2.2 exponential_divide_fusion.2
  203.8 1.3 copy-done.1
  207.7 3.0 %fusion.101 = f32[1,256,8,64]{1,3,2,0:T(8,128)} fusion(bf16[512,8,64]{0,2,1:T(8,128)(2,1)} %bitcast.227, bf16[8,512,256]{2,1,0:T(8,128)(2,1)} %copy-done.1, f32[1,256,8,64]{1,3,2,0:T(8,128)} %get-tuple-element.620, pred[]{:T(512)S(6)} %compare.19), kind=kOutput, calls=%fused_computation.27.clone.1 | convolution fusion | flops 134610944 | bytes 3670017 | tf_op jit(solution)/shard_map/while/body/eval_jaxpr/chfk,ckhe->cfhe/dot_general | solution.py:151
  212.0 1.3 constant_dynamic-slice_fusion.10
  213.3 2.2 exponential_divide_fusion.2
  216.3 1.3 copy-done.1
  220.2 3.1 %fusion.101 = f32[1,256,8,64]{1,3,2,0:T(8,128)} fusion(bf16[512,8,64]{0,2,1:T(8,128)(2,1)} %bitcast.227, bf16[8,512,256]{2,1,0:T(8,128)(2,1)} %copy-done.1, f32[1,256,8,64]{1,3,2,0:T(8,128)} %get-tuple-element.620, pred[]{:T(512)S(6)} %compare.19), kind=kOutput, calls=%fused_computation.27.clone.1 | convolution fusion | flops 134610944 | bytes 3670017 | tf_op jit(solution)/shard_map/while/body/eval_jaxpr/chfk,ckhe->cfhe/dot_general | solution.py:151
  223.3 3.3 %copy.58 = bf16[2,1,128,8,512]{4,3,0,2,1:T(8,128)(2,1)} copy(bf16[2,1,128,8,512]{4,3,2,1,0:T(8,128)(2,1)} %bitcast.70) | data formatting | bytes 4194304 | tf_op jit(solution)/shard_map/reshape | solution.py:171
  227.7 40.2 %reduce-scatter.2.cloned.1.call-done = bf16[256,1,1024]{0,2,1:T(8,128)(2,1)} async-done(((bf16[1024,1,1024]{0,2,1:T(8,128)(2,1)}), bf16[256,1,1024]{0,2,1:T(8,128)(2,1)}) %reduce-scatter.2.cloned.1.call-update) | async-done | bytes 524304 | tf_op jit(solution)/shard_map/reduce_scatter | solution.py:172
  269.9 2.3 copy.56
  (84 shorter events, 23.3 us)
Async XLA Ops:
  7.2 71.4 %copy-start = (bf16[1024,3,512]{2,0,1:T(8,128)(2,1)S(1)}, bf16[1024,3,512]{2,0,1:T(8,128)(2,1)}, u32[]{:S(2)}) copy-start(bf16[1024,3,512]{2,0,1:T(8,128)(2,1)} %param.17) | copy-start | bytes 9437188
  7.2 103.2 %all-gather.5.cloned.1.call-start = ((), (), s32[]{:S(2)}) async-start(), calls=%async_computation.2 | async-start | bytes 1310720 | tf_op jit(solution)/shard_map/all_gather | solution.py:71
  15.8 1.0 copy-start.5
  17.0 9.6 %collective-permute-start = (bf16[1,256,4]{2,1,0:T(8,128)(2,1)S(1)}, bf16[1,256,4]{2,1,0:T(8,128)(2,1)S(1)}, u32[]{:S(2)}, u32[]{:S(2)}) collective-permute-start(bf16[1,256,4]{2,1,0:T(8,128)(2,1)S(1)} %get-tuple-element.365), channel_id=1, source_target_pairs={{0,4},{4,8},{8,12},{1,5},{5,9},{9,13},{2,6},{6,10},{10,14},{3,7},{... | collective-permute-start | bytes 6152 | tf_op jit(solution)/shard_map/ppermute | solution.py:18
  21.9 6.2 %collective-permute-start.1 = (bf16[1,256,4]{2,1,0:T(8,128)(2,1)S(1)}, bf16[1,256,4]{2,1,0:T(8,128)(2,1)S(1)}, u32[]{:S(2)}, u32[]{:S(2)}) collective-permute-start(bf16[1,256,4]{2,1,0:T(8,128)(2,1)S(1)} %get-tuple-element.364), channel_id=1, source_target_pairs={{4,0},{8,4},{12,8},{5,1},{9,5},{13,9},{6,2},{10,6},{14,10},{7,3},{... | collective-permute-start | bytes 6152 | tf_op jit(solution)/shard_map/ppermute | solution.py:21
  61.7 1.9 copy-start.6
  70.4 0.7 copy-start.7
  78.6 2.1 copy-start.9
  80.6 58.8 %all-gather.7.cloned.1.call-start = ((), (), s32[]{:S(2)}) async-start(), calls=%async_computation.3 | async-start | bytes 1310720 | tf_op jit(solution)/shard_map/all_gather | solution.py:72
  81.8 186.0 %reduce-scatter.2.cloned.1.call-start = ((), (), s32[]{:S(2)}) async-start(), calls=%async_computation.1 | async-start | bytes 2621440 | tf_op jit(solution)/shard_map/reduce_scatter | solution.py:172
  141.7 16.1 %copy-start.8 = (f32[512]{0:T(512)S(1)}, f32[512]{0:T(512)}, u32[]{:S(2)}) copy-start(f32[512]{0:T(512)} %param.18) | copy-start | bytes 6148
  141.7 50.6 %copy-start.10 = (s32[4]{0:T(128)S(1)}, s32[4]{0:T(128)}, u32[]{:S(2)}) copy-start(s32[4]{0:T(128)} %param.21) | copy-start | bytes 52
  155.6 38.7 %copy-start.3 = (bf16[1,256,8,64]{1,3,2,0:T(8,128)(2,1)}, bf16[1,256,8,64]{1,3,2,0:T(8,128)(2,1)S(1)}, u32[]{:S(2)}) copy-start(bf16[1,256,8,64]{1,3,2,0:T(8,128)(2,1)S(1)} %get-tuple-element.656) | copy-start | bytes 786436
  192.2 6.1 %copy-start.11 = (f32[2]{0:T(128)}, f32[2]{0:T(128)S(1)}, u32[]{:S(2)}) copy-start(f32[2]{0:T(128)S(1)} %psum.7) | copy-start | bytes 28
  200.8 2.2 copy-start.2
  203.0 2.1 copy-start.4
  203.8 1.3 copy-start.1
  213.3 2.2 copy-start.2
  215.5 2.1 copy-start.4
  216.3 1.3 copy-start.1
Sparse Core Ops, SparseCore 0:
  80.7 29.6 all-gather.4
  111.9 27.4 all-gather.6
  226.7 41.0 reduce-scatter.1
where the time goes:
time: 280 us; the launch traced here: 279 us
  waiting for transfers between devices  80.7 us (29%)
  local copies, waits for them, and re-layouts  71.9 us (26%)
  blocking collectives  39.2 us (14%)
  other arithmetic  31.1 us (11%)
  matrix products  29.7 us (11%)
  between operations  15.3 us (5%)
  starting transfers between devices  6.74 us (2%)
  loops' own time  4.08 us (1%)
    reduce_scatter x1, waiting for transfers between devices, local(): lax.psum_scatter(stacked.astype(f32).astype(jnp.bfloat16), 'seq', scatter...  40.2 us
    psum x1, blocking collectives, local(): lax.psum(jnp.sum(owner * partial_rewards[:, None], axis=0), ('seq', 'mp',...  31.9 us
    all_gather x1, waiting for transfers between devices, local(): lax.all_gather(qkv[:, :, 1], 'seq', axis=1, tiled=True)  28.3 us
    slice x2, local copies, waits for them, and re-layouts, local(): blocks[:, :, :-1]  14.2 us
    all_gather x1, waiting for transfers between devices, local(): lax.all_gather(qkv[:, :, 2], 'seq', axis=1, tiled=True)  10.6 us
    dot_general x4, matrix products, scores_for(): jnp.einsum('cfhe,ckhe->chfk', query4, key_slice(keys, start, size), prefe...  9.74 us
    dynamic_slice x6, local copies, waits for them, and re-layouts, key_slice(): lax.dynamic_slice_in_dim(source, start, size, 1)  9.22 us
    unnamed x21, local copies, waits for them, and re-layouts  8.64 us
  transfers between devices with their start and end apart: 5, of which 4 were waited for; matrix products, arithmetic and copies ran while one was open for 8% of the time, Pallas kernels for 0%

commit v1 on v0

--- a/solution.py
+++ b/solution.py
@@ -125,7 +125,9 @@
         == (section_id * cand + jnp.arange(cand, dtype=jnp.int32))[:, None]
     ).astype(f32)
     partial_rewards = jnp.sum(attended * gate * readout, axis=(1, 2)) / math.sqrt(total)
-    rewards = lax.psum(jnp.sum(owner * partial_rewards[:, None], axis=0), ("seq", "mp", "section"))
+    rewards = jnp.sum(owner * partial_rewards[:, None], axis=0)
+    for over in (("mp", "section"), "seq"):
+        rewards = lax.psum(rewards, over)
     chosen = (pairs[:, :, None] == jnp.arange(all_cands, dtype=jnp.int32)[None, None, :]).astype(
         f32
     )

time: 280 us -> 266 us (0.950)
  blocking collectives: 39.2 us -> 24.4 us
    psum x1 -> x2, blocking collectives: 31.9 us -> 17.1 us  [local(): rewards = lax.psum(rewards, over)]
where the time goes in v1:
time: 266 us; the launch traced here: 264 us
  waiting for transfers between devices  81 us (30%)
  local copies, waits for them, and re-layouts  72 us (27%)
  other arithmetic  31.2 us (12%)
  matrix products  29.7 us (11%)
  blocking collectives  24.4 us (9%)
  between operations  15.3 us (6%)
  starting transfers between devices  6.74 us (3%)
  loops' own time  4.19 us (2%)
    reduce_scatter x1, waiting for transfers between devices, local(): lax.psum_scatter(stacked.astype(f32).astype(jnp.bfloat16), 'seq', scatter...  40.2 us
    all_gather x1, waiting for transfers between devices, local(): lax.all_gather(qkv[:, :, 1], 'seq', axis=1, tiled=True)  28.3 us
    psum x2, blocking collectives, local(): rewards = lax.psum(rewards, over)  17.1 us
    slice x2, local copies, waits for them, and re-layouts, local(): blocks[:, :, :-1]  14.2 us
    all_gather x1, waiting for transfers between devices, local(): lax.all_gather(qkv[:, :, 2], 'seq', axis=1, tiled=True)  11 us
    dot_general x4, matrix products, scores_for(): jnp.einsum('cfhe,ckhe->chfk', query4, key_slice(keys, start, size), prefe...  9.71 us
    dynamic_slice x6, local copies, waits for them, and re-layouts, key_slice(): lax.dynamic_slice_in_dim(source, start, size, 1)  9.18 us
    unnamed x21, local copies, waits for them, and re-layouts  8.66 us
  transfers between devices with their start and end apart: 5, of which 4 were waited for; matrix products, arithmetic and copies ran while one was open for 8% of the time, Pallas kernels for 0%

profile of v1, /device:TPU:0, one launch (start us, length us, event | category | flops | bytes accessed | tf_op | source)
XLA Modules:
  0.0 264.4 jit_solution(8172814715798387354)
XLA Ops:
  7.2 8.6 %fusion.25 = bf16[1,256,2048]{2,1,0:T(8,128)(2,1)S(1)} fusion(bf16[1,256,2048]{2,1,0:T(8,128)(2,1)} %param.14, f32[256]{0:T(256)} %param.15), kind=kLoop, calls=%fused_computation.40 | loop fusion | flops 3145728 | bytes 2098176 | tf_op jit(solution)/shard_map/convert_element_type | solution.py:46
  17.0 4.9 %collective-permute-start = (bf16[1,256,4]{2,1,0:T(8,128)(2,1)S(1)}, bf16[1,256,4]{2,1,0:T(8,128)(2,1)S(1)}, u32[]{:S(2)}, u32[]{:S(2)}) collective-permute-start(bf16[1,256,4]{2,1,0:T(8,128)(2,1)S(1)} %get-tuple-element.365), channel_id=1, source_target_pairs={{0,4},{4,8},{8,12},{1,5},{5,9},{9,13},{2,6},{6,10},{10,14},{3,7},{... | collective-permute-start | bytes 6152 | tf_op jit(solution)/shard_map/ppermute | solution.py:18
  21.9 1.5 collective-permute-start.1
  24.1 2.4 reshape.438
  26.5 1.5 collective-permute-done.1
  28.1 3.5 %concatenate.32 = bf16[1,256,2056]{2,1,0:T(8,128)(2,1)} concatenate(bf16[1,256,4]{2,1,0:T(8,128)(2,1)S(1)} %collective-permute-done, bf16[1,256,2048]{2,1,0:T(8,128)(2,1)} %copy-done.5, bf16[1,256,4]{2,1,0:T(8,128)(2,1)S(1)} %collective-permute-done.1), dimensions={2} | concatenate | bytes 2105344 | tf_op jit(solution)/shard_map/concatenate | solution.py:22
  31.5 2.3 copy.41
  33.9 5.8 %reshape.436 = bf16[1,8,32,257,8]{2,1,4,3,0:T(8,128)(2,1)} reshape(bf16[1,256,2056]{1,2,0:T(8,128)(2,1)} %copy.41) | data formatting | bytes 2105344 | tf_op jit(solution)/shard_map/reshape | solution.py:48
  39.7 6.5 %fusion.53 = (bf16[1,8,256,32,8]{3,1,4,2,0:T(8,128)(2,1)}, bf16[1,8,256,32,8]{3,1,4,2,0:T(8,128)(2,1)}) fusion(bf16[1,8,257,32,8]{3,1,4,2,0:T(8,128)(2,1)} %bitcast.233), kind=kLoop, calls=%fused_computation.102 | loop fusion | bytes 4194304 | tf_op jit(solution)/shard_map/slice | solution.py:51
  46.2 7.7 %copy.42 = bf16[1,8,256,32,8]{2,4,3,1,0:T(8,128)(2,1)} copy(bf16[1,8,256,32,8]{3,1,4,2,0:T(8,128)(2,1)} %get-tuple-element.362) | data formatting | bytes 2097152 | tf_op jit(solution)/shard_map/slice | solution.py:51
  53.9 7.8 %copy.43 = bf16[1,8,256,32,8]{2,4,3,1,0:T(8,128)(2,1)} copy(bf16[1,8,256,32,8]{3,1,4,2,0:T(8,128)(2,1)} %get-tuple-element.363) | data formatting | bytes 2097152 | tf_op jit(solution)/shard_map/slice | solution.py:51
  61.7 1.8 pad_maximum_fusion
  63.5 1.3 fusion.27
  64.9 2.0 copy.46
  66.9 3.5 %fusion.31 = bf16[1,256,512]{2,1,0:T(8,128)(2,1)S(1)} fusion(f32[1,256,512]{2,1,0:T(8,128)} %copy.46, f32[512]{0:T(512)S(1)} %fusion.36, f32[256]{0:T(256)S(1)} %add_convert_fusion, pred[512]{0:T(512)(128)(4,1)S(1)} %fusion.33), kind=kLoop, calls=%fused_computation.52 | loop fusion | flops 524288 | bytes 790016 | tf_op jit(solution)/shard_map/convert_element_type | solution.py:64
  71.1 7.3 %all_gather.9 = bf16[1,256,1024]{2,1,0:T(8,128)(2,1)S(1)} all-gather(bf16[1,256,512]{2,1,0:T(8,128)(2,1)S(1)} %fusion.31), channel_id=1, replica_groups=mesh['groups'=2,'seq'=4,'mp'=2,'section'=2] {'mp'}, dimensions={2}, use_global_device_ids=true | all-gather | bytes 786432 | tf_op jit(solution)/shard_map/all_gather | solution.py:65
  82.0 28.3 %all-gather.5.cloned.1.call-done = bf16[1,1024,1,512]{3,1,2,0:T(8,128)(2,1)} async-done(((bf16[1,256,1,512]{3,1,2,0:T(8,128)(2,1)}), bf16[1,1024,1,512]{3,1,2,0:T(8,128)(2,1)}) %all-gather.5.cloned.1.call-update) | async-done | bytes 1048592 | tf_op jit(solution)/shard_map/all_gather | solution.py:71
  110.3 2.3 copy.53
  112.6 16.3 %while.37 = (s32[]{:T(128)}, f32[1,8,256]{2,1,0:T(8,128)S(1)}, f32[1,8,256]{2,1,0:T(8,128)S(1)}, s32[2]{0:T(128)S(1)}, bf16[1,1024,512]{1,2,0:T(8,128)(2,1)}, /*...) while((s32[]{:T(128)}, f32[1,8,256]{2,1,0:T(8,128)S(1)}, ...), condition=%wide.region_4.5_spmd.clone, body=%wide.region_1.4_spmd.clone.sunk | while | flops 139470848 | bytes 10330286 | solution.py:101
  115.0 2.7 %bitcast_reduce_fusion.2 = (f32[8,256]{1,0:T(8,128)S(1)}, f32[8,512,256]{2,1,0:T(8,128)}) fusion(bf16[512,8,64]{0,2,1:T(8,128)(2,1)S(1)} %bitcast.228, bf16[1,256,8,64]{1,3,2,0:T(8,128)(2,1)S(1)} %get-tuple-element.563), kind=kOutput, calls=%fused_computation.1.clone.1 | convolution fusion | flops 136312832 | bytes 4988928 | tf_op jit(solution)/shard_map/while/body/eval_jaxpr/cfhe,ckhe->chfk/dot_general | solution.py:85
  117.7 3.0 %fusion.86 = f32[8,256]{1,0:T(8,128)S(1)} fusion(f32[8,512,256]{2,1,0:T(8,128)} %get-tuple-element.514, f32[8,256]{1,0:T(8,128)S(1)} %bitcast.239), kind=kLoop, calls=%fused_computation.3.clone.1 | loop fusion | flops 3143680 | bytes 4210688 | tf_op jit(solution)/shard_map/while/body/eval_jaxpr/reduce_sum | solution.py:95
  123.3 2.7 %bitcast_reduce_fusion.2 = (f32[8,256]{1,0:T(8,128)S(1)}, f32[8,512,256]{2,1,0:T(8,128)}) fusion(bf16[512,8,64]{0,2,1:T(8,128)(2,1)S(1)} %bitcast.228, bf16[1,256,8,64]{1,3,2,0:T(8,128)(2,1)S(1)} %get-tuple-element.563), kind=kOutput, calls=%fused_computation.1.clone.1 | convolution fusion | flops 136312832 | bytes 4988928 | tf_op jit(solution)/shard_map/while/body/eval_jaxpr/cfhe,ckhe->chfk/dot_general | solution.py:85
  126.0 2.9 %fusion.86 = f32[8,256]{1,0:T(8,128)S(1)} fusion(f32[8,512,256]{2,1,0:T(8,128)} %get-tuple-element.514, f32[8,256]{1,0:T(8,128)S(1)} %bitcast.239), kind=kLoop, calls=%fused_computation.3.clone.1 | loop fusion | flops 3143680 | bytes 4210688 | tf_op jit(solution)/shard_map/while/body/eval_jaxpr/reduce_sum | solution.py:95
  128.9 11.0 %all-gather.7.cloned.1.call-done = bf16[1,1024,1,512]{3,1,2,0:T(8,128)(2,1)} async-done(((bf16[1,256,1,512]{3,1,2,0:T(8,128)(2,1)}), bf16[1,1024,1,512]{3,1,2,0:T(8,128)(2,1)}) %all-gather.7.cloned.1.call-update) | async-done | bytes 1048592 | tf_op jit(solution)/shard_map/all_gather | solution.py:72
  139.9 2.3 copy.54
  142.2 13.9 %while.38 = (s32[]{:T(128)}, f32[1,256,8,64]{1,3,2,0:T(8,128)}, s32[2]{0:T(128)S(1)}, bf16[1,1024,512]{1,2,0:T(8,128)(2,1)}, bf16[1,1024,512]{1,2,0:T(8,128)(2,1...) while((s32[]{:T(128)}, f32[1,256,8,64]{1,3,2,0:T(8,128)}, ...), condition=%wide.region_6.7_spmd.clone, body=%wide.region_5.6_spmd.clone.sunk | while | flops 272891904 | bytes 4473021 | solution.py:116
  143.4 2.2 constant_dynamic-slice_fusion.9
  145.7 3.4 %fusion.90 = f32[1,256,8,64]{1,3,2,0:T(8,128)} fusion(bf16[512,8,64]{0,2,1:T(8,128)(2,1)} %bitcast.236, bf16[512,8,64]{0,2,1:T(8,128)(2,1)} %bitcast.235, f32[8,256]{1,0:T(8,128)S(1)} %bitcast.249, f32[8,256]{1,0:T(8,128)S(1)} %bitcast.245, f32[1,256,8,64]{1,3,2,0:T(8,128)} %get-tuple-element.581, ...), kind=kOutput, calls=%fused_computation.13.clone.1 | convolution fusion | flops 272891904 | bytes 2375681 | tf_op jit(solution)/shard_map/while/body/eval_jaxpr/chfk,ckhe->cfhe/dot_general | solution.py:111
  150.3 2.2 constant_dynamic-slice_fusion.9
  152.5 3.5 %fusion.90 = f32[1,256,8,64]{1,3,2,0:T(8,128)} fusion(bf16[512,8,64]{0,2,1:T(8,128)(2,1)} %bitcast.236, bf16[512,8,64]{0,2,1:T(8,128)(2,1)} %bitcast.235, f32[8,256]{1,0:T(8,128)S(1)} %bitcast.249, f32[8,256]{1,0:T(8,128)S(1)} %bitcast.245, f32[1,256,8,64]{1,3,2,0:T(8,128)} %get-tuple-element.581, ...), kind=kOutput, calls=%fused_computation.13.clone.1 | convolution fusion | flops 272891904 | bytes 2375681 | tf_op jit(solution)/shard_map/while/body/eval_jaxpr/chfk,ckhe->cfhe/dot_general | solution.py:111
  156.1 2.1 copy.51
  158.2 1.9 multiply_reduce_fusion.2
  160.8 6.4 %psum.14 = f32[2]{0:T(128)S(1)} all-reduce(f32[2]{0:T(128)S(1)} %compare_select_fusion.2), channel_id=1, replica_groups=mesh['groups'=2,'seq'=4,'mp'=2,'section'=2] {'mp','section'}, use_global_device_ids=true, to_apply=%region_8.9 | all-reduce | flops 2 | bytes 16 | tf_op jit(solution)/shard_map/psum | solution.py:130
  167.2 10.7 %psum.15 = f32[2]{0:T(128)S(1)} all-reduce(f32[2]{0:T(128)S(1)} %psum.14), channel_id=1, replica_groups=mesh['groups'=2,'seq'=4,'mp'=2,'section'=2] {'seq'}, use_global_device_ids=true, to_apply=%region_9.10 | all-reduce | flops 2 | bytes 16 | tf_op jit(solution)/shard_map/psum | solution.py:130
  179.9 1.8 multiply_convert_fusion.2
  182.8 1.1 multiply_reduce_fusion.1
  184.0 25.0 %while.39 = (s32[]{:T(128)}, f32[1,256,8,64]{1,3,2,0:T(8,128)}, bf16[2,512,1,1024]{1,3,2,0:T(8,128)(2,1)}, s32[2]{0:T(128)S(1)}, bf16[1,1024,512]{1,2,0:T(8,128)...) while((s32[]{:T(128)}, f32[1,256,8,64]{1,3,2,0:T(8,128)}, ...), condition=%wide.region_15.16_spmd.clone, body=%wide.region_14.15_spmd.clone.sunk | while | flops 681705472 | bytes 39346984 | solution.py:172
  185.2 1.3 constant_dynamic-slice_fusion.10
  186.5 2.2 exponential_divide_fusion.2
  189.5 1.3 copy-done.1
  193.4 3.0 %fusion.101 = f32[1,256,8,64]{1,3,2,0:T(8,128)} fusion(bf16[512,8,64]{0,2,1:T(8,128)(2,1)} %bitcast.227, bf16[8,512,256]{2,1,0:T(8,128)(2,1)} %copy-done.1, f32[1,256,8,64]{1,3,2,0:T(8,128)} %get-tuple-element.620, pred[]{:T(512)S(6)} %compare.19), kind=kOutput, calls=%fused_computation.27.clone.1 | convolution fusion | flops 134610944 | bytes 3670017 | tf_op jit(solution)/shard_map/while/body/eval_jaxpr/chfk,ckhe->cfhe/dot_general | solution.py:153
  197.7 1.3 constant_dynamic-slice_fusion.10
  199.0 2.2 exponential_divide_fusion.2
  202.0 1.3 copy-done.1
  205.9 3.1 %fusion.101 = f32[1,256,8,64]{1,3,2,0:T(8,128)} fusion(bf16[512,8,64]{0,2,1:T(8,128)(2,1)} %bitcast.227, bf16[8,512,256]{2,1,0:T(8,128)(2,1)} %copy-done.1, f32[1,256,8,64]{1,3,2,0:T(8,128)} %get-tuple-element.620, pred[]{:T(512)S(6)} %compare.19), kind=kOutput, calls=%fused_computation.27.clone.1 | convolution fusion | flops 134610944 | bytes 3670017 | tf_op jit(solution)/shard_map/while/body/eval_jaxpr/chfk,ckhe->cfhe/dot_general | solution.py:153
  209.0 3.3 %copy.58 = bf16[2,1,128,8,512]{4,3,0,2,1:T(8,128)(2,1)} copy(bf16[2,1,128,8,512]{4,3,2,1,0:T(8,128)(2,1)} %bitcast.70) | data formatting | bytes 4194304 | tf_op jit(solution)/shard_map/reshape | solution.py:173
  213.4 40.2 %reduce-scatter.2.cloned.1.call-done = bf16[256,1,1024]{0,2,1:T(8,128)(2,1)} async-done(((bf16[1024,1,1024]{0,2,1:T(8,128)(2,1)}), bf16[256,1,1024]{0,2,1:T(8,128)(2,1)}) %reduce-scatter.2.cloned.1.call-update) | async-done | bytes 524304 | tf_op jit(solution)/shard_map/reduce_scatter | solution.py:174
  255.6 2.3 copy.56
  (85 shorter events, 24.4 us)
Async XLA Ops:
  7.2 71.4 %copy-start = (bf16[1024,3,512]{2,0,1:T(8,128)(2,1)S(1)}, bf16[1024,3,512]{2,0,1:T(8,128)(2,1)}, u32[]{:S(2)}) copy-start(bf16[1024,3,512]{2,0,1:T(8,128)(2,1)} %param.17) | copy-start | bytes 9437188
  7.2 103.1 %all-gather.5.cloned.1.call-start = ((), (), s32[]{:S(2)}) async-start(), calls=%async_computation.2 | async-start | bytes 1310720 | tf_op jit(solution)/shard_map/all_gather | solution.py:71
  15.8 1.0 copy-start.5
  17.0 9.6 %collective-permute-start = (bf16[1,256,4]{2,1,0:T(8,128)(2,1)S(1)}, bf16[1,256,4]{2,1,0:T(8,128)(2,1)S(1)}, u32[]{:S(2)}, u32[]{:S(2)}) collective-permute-start(bf16[1,256,4]{2,1,0:T(8,128)(2,1)S(1)} %get-tuple-element.365), channel_id=1, source_target_pairs={{0,4},{4,8},{8,12},{1,5},{5,9},{9,13},{2,6},{6,10},{10,14},{3,7},{... | collective-permute-start | bytes 6152 | tf_op jit(solution)/shard_map/ppermute | solution.py:18
  21.9 6.2 %collective-permute-start.1 = (bf16[1,256,4]{2,1,0:T(8,128)(2,1)S(1)}, bf16[1,256,4]{2,1,0:T(8,128)(2,1)S(1)}, u32[]{:S(2)}, u32[]{:S(2)}) collective-permute-start(bf16[1,256,4]{2,1,0:T(8,128)(2,1)S(1)} %get-tuple-element.364), channel_id=1, source_target_pairs={{4,0},{8,4},{12,8},{5,1},{9,5},{13,9},{6,2},{10,6},{14,10},{7,3},{... | collective-permute-start | bytes 6152 | tf_op jit(solution)/shard_map/ppermute | solution.py:21
  61.7 1.9 copy-start.6
  70.4 0.7 copy-start.7
  78.6 2.0 copy-start.9
  80.5 59.4 %all-gather.7.cloned.1.call-start = ((), (), s32[]{:S(2)}) async-start(), calls=%async_computation.3 | async-start | bytes 1310720 | tf_op jit(solution)/shard_map/all_gather | solution.py:72
  81.8 171.8 %reduce-scatter.2.cloned.1.call-start = ((), (), s32[]{:S(2)}) async-start(), calls=%async_computation.1 | async-start | bytes 2621440 | tf_op jit(solution)/shard_map/reduce_scatter | solution.py:174
  142.2 16.0 %copy-start.8 = (f32[512]{0:T(512)S(1)}, f32[512]{0:T(512)}, u32[]{:S(2)}) copy-start(f32[512]{0:T(512)} %param.18) | copy-start | bytes 6148
  142.2 35.7 %copy-start.10 = (s32[4]{0:T(128)S(1)}, s32[4]{0:T(128)}, u32[]{:S(2)}) copy-start(s32[4]{0:T(128)} %param.21) | copy-start | bytes 52
  156.1 23.9 %copy-start.3 = (bf16[1,256,8,64]{1,3,2,0:T(8,128)(2,1)}, bf16[1,256,8,64]{1,3,2,0:T(8,128)(2,1)S(1)}, u32[]{:S(2)}) copy-start(bf16[1,256,8,64]{1,3,2,0:T(8,128)(2,1)S(1)} %get-tuple-element.656) | copy-start | bytes 786436
  177.8 6.1 %copy-start.11 = (f32[2]{0:T(128)}, f32[2]{0:T(128)S(1)}, u32[]{:S(2)}) copy-start(f32[2]{0:T(128)S(1)} %psum.15) | copy-start | bytes 28
  186.5 2.2 copy-start.2
  188.7 2.1 copy-start.4
  189.5 1.4 copy-start.1
  199.0 2.2 copy-start.2
  201.2 2.1 copy-start.4
  202.0 1.4 copy-start.1
Sparse Core Ops, SparseCore 0:
  80.7 29.5 all-gather.4
  112.4 27.4 all-gather.6
  212.4 41.0 reduce-scatter.1
